TPU v7x, 128 devices: a whole 4x4x4 slice. The times are simulated.
128 devices in a mesh: dir: 4 (over z_hi, core), space: 32 (over y, x, z_lo).
Axes of the slice: x: 4, y: 4, z: 4 (z_hi: 2, z_lo: 2; z = z_hi * 2 + z_lo), core: 2. Of those that a mesh axis runs over, the one named last changes fastest.
Arguments:
- store: float32 [4, 2, 128, 512, 128], P('dir', None, 'space'), may hold values from 0.2 to 1.5
- rate: float32 [128, 512, 128], P('space'), may hold values from 0.3 to 3
- directions: float32 [8, 32, 8192], P('dir', 'space'), may hold values from -6 to 6
- owner_map: int32 [4], replicated, may hold values from 0 to 3, each once
- block_map: int32 [32], replicated, may hold values from 0 to 31, each once
Outputs:
- tangent: float32 [8, 2, 128, 512, 128], P('dir', None, 'space')
- sens: float32 [8, 32, 8192], P('dir', 'space')
All inputs are finite; a program needn't handle non-finite values.
Results may differ from a plain program's by a relative error of at most 0.000071.
Values sent between devices are 32-bit elements; how exact they have to be, the bound alone decides.
A program may use at most 192 MiB of HBM per device.

v0:
```python
import jax
import jax.numpy as jnp
from jax import lax
from jax.sharding import PartitionSpec as P

STEPS = 2
SUBSTEPS = 3


spread_a = 0.08
spread_b = 0.06
drift = 0.25
decay_rate = 0.05
rate_scale = 0.1


def spread(value, axis, source):
    kept = jnp.where(lax.axis_index(axis) == source, value, 0).astype(value.dtype)
    return lax.psum(kept, axis)


def padded(block, sides, width):
    for axis, dim in sides:
        count = lax.axis_size(axis)
        forward = [(i, i + 1) for i in range(count - 1)]
        backward = [(target, source) for source, target in forward]
        low = lax.ppermute(
            lax.slice_in_dim(block, block.shape[dim] - width, None, axis=dim), axis, forward
        )
        high = lax.ppermute(lax.slice_in_dim(block, 0, width, axis=dim), axis, backward)
        block = jnp.concatenate([low, block, high], axis=dim)
    return block


def across_yz(field):
    lead = ((0, 0),) * (field.ndim - 2)
    total = jnp.pad(field[..., 1:, :], lead + ((0, 1), (0, 0)))
    total = total + jnp.pad(field[..., :-1, :], lead + ((1, 0), (0, 0)))
    total = total + jnp.pad(field[..., :, 1:], lead + ((0, 0), (0, 1)))
    total = total + jnp.pad(field[..., :, :-1], lead + ((0, 0), (1, 0)))
    return total


def advance(
    first, first_lower, first_upper, second, second_lower, second_upper, conc_a, conc_b, rate, vfine
):
    lap_first = first_lower + first_upper + across_yz(first) - 6.0 * first
    lap_second = second_lower + second_upper + across_yz(second) - 6.0 * second
    source = rate_scale * rate * (vfine * conc_a * conc_b + first * conc_b + conc_a * second)
    first_new = first + spread_a * lap_first - drift * (first - first_lower) - source
    second_new = (
        second
        + spread_b * lap_second
        - drift * (second - second_lower)
        + source
        - decay_rate * second
    )
    return (first_new, second_new)


def local(store, rate, directions, owner_map, block_map):
    dirs_dev = directions.shape[0]
    width_x, width_y, width_z = rate.shape
    mine = lax.axis_index("space")
    n_space = lax.axis_size("space")
    every = lax.all_gather(directions, "space", axis=1, tiled=True)
    clipped = jnp.clip(mine, 0, n_space - 1)
    picked_row = lax.dynamic_index_in_dim(every, block_map[clipped], 1, keepdims=False)
    coarse_one = picked_row.reshape(dirs_dev, width_x // 2, width_y // 4, width_z // 4)
    fine_one = jnp.repeat(jnp.repeat(jnp.repeat(coarse_one, 2, 1), 4, 2), 4, 3)
    valid = ((mine >= 0) & (mine < n_space)).astype(jnp.float32)
    vfine = fine_one * valid
    first = jnp.zeros((dirs_dev, width_x, width_y, width_z), jnp.float32)
    second = jnp.zeros((dirs_dev, width_x, width_y, width_z), jnp.float32)
    for step in range(STEPS):
        slab = spread(store, "dir", owner_map[step])[0]
        for inner in range(SUBSTEPS):
            edges = jnp.stack(
                [
                    jnp.concatenate([first[:, :1], first[:, -1:]], 1),
                    jnp.concatenate([second[:, :1], second[:, -1:]], 1),
                ],
                0,
            )
            wide = padded(edges, (("space", 2),), 1)
            first_lower = jnp.concatenate([wide[0, :, 0:1], first[:, :-1]], 1)
            first_upper = jnp.concatenate([first[:, 1:], wide[0, :, 3:4]], 1)
            second_lower = jnp.concatenate([wide[1, :, 0:1], second[:, :-1]], 1)
            second_upper = jnp.concatenate([second[:, 1:], wide[1, :, 3:4]], 1)
            first, second = advance(
                first,
                first_lower,
                first_upper,
                second,
                second_lower,
                second_upper,
                slab[0],
                slab[1],
                rate,
                vfine,
            )
    tangent = jnp.stack([first, second], 1)
    means = second.reshape(dirs_dev, width_x // 2, 2, width_y // 4, 4, width_z // 4, 4).mean(
        axis=(2, 4, 6)
    )
    coarse_q = means.reshape(dirs_dev, 1, -1)
    gathered = lax.all_gather(coarse_q, "space", axis=1, tiled=True)
    weights = (block_map == mine).astype(jnp.float32)
    sens = jnp.einsum("s,dsc->dc", weights, gathered, precision=lax.Precision.HIGHEST)[:, None]
    return (tangent, sens)


def solution(mesh):
    return jax.shard_map(
        local,
        mesh=mesh,
        in_specs=(
            P("dir", None, "space", None, None),
            P("space", None, None),
            P("dir", "space", None),
            P(),
            P(),
        ),
        out_specs=(P("dir", None, "space", None, None), P("dir", "space", None)),
        check_vma=False,
    )
```

profile of v0, /device:TPU:0, one launch (start us, length us, event | category | flops | bytes accessed | tf_op | source)
XLA Modules:
  0.0 876.8 jit_solution(12691227692736969560)
XLA Ops:
  12.3 4.1 broadcast_select_fusion
  18.3 5.5 collective-permute-start
  26.7 37.1 %collective-permute-done.1 = f32[2,2,1,512,128]{3,2,4,1,0:T(1,128)} collective-permute-done((f32[2,2,1,512,128]{3,2,4,1,0:T(1,128)S(1)}, f32[2,2,1,512,128]{3,2,4,1,0:T(1,128)}, u32[]{:S(2)}, u32[]{:S(2)}) %collective-permute-start.1) | collective-permute-done | bytes 1048608 | tf_op jit(solution)/shard_map/ppermute | solution.py:30
  63.8 3.0 slice_bitcast_fusion.26
  66.8 25.2 %collective-permute-done = f32[2,2,1,512,128]{3,2,4,1,0:T(1,128)} collective-permute-done((f32[2,2,1,512,128]{3,2,4,1,0:T(1,128)S(1)}, f32[2,2,1,512,128]{3,2,4,1,0:T(1,128)}, u32[]{:S(2)}, u32[]{:S(2)}) %collective-permute-start) | collective-permute-done | bytes 1048608 | tf_op jit(solution)/shard_map/ppermute | solution.py:27
  92.0 2.9 slice_bitcast_fusion.27
  94.9 151.8 %all-gather.3.cloned.1.call-done = f32[2,32,8192]{2,0,1:T(2,128)} async-done(((f32[2,1,8192]{2,0,1:T(2,128)}), f32[2,32,8192]{2,0,1:T(2,128)}) %all-gather.3.cloned.1.call-update) | async-done | bytes 2097168 | tf_op jit(solution)/shard_map/all_gather | solution.py:66
  249.6 3.2 broadcast_multiply_fusion.1
  252.7 2.0 slice_bitcast_fusion.1
  254.8 2.7 copy.87
  257.5 2.7 copy.86
  266.5 4.9 fusion.3
  272.2 2.6 fusion.118
  274.8 3.4 fusion.117
  278.2 2.8 fusion.119
  283.7 2.6 fusion.82
  286.4 6.3 collective-permute-start.2
  294.2 2.6 fusion.122
  296.8 2.7 copy.89
  299.5 2.6 copy.90
  302.1 3.8 fusion.121
  306.8 13.4 %collective-permute-done.2 = f32[2,2,1,512,128]{3,2,4,1,0:T(1,128)} collective-permute-done((f32[2,2,1,512,128]{3,2,4,1,0:T(1,128)}, f32[2,2,1,512,128]{3,2,4,1,0:T(1,128)}, u32[]{:S(2)}, u32[]{:S(2)}) %collective-permute-start.2) | collective-permute-done | bytes 1048608 | tf_op jit(solution)/shard_map/ppermute | solution.py:27
  320.2 1.9 slice_bitcast_fusion.23
  322.1 2.7 slice_bitcast_fusion.22
  324.9 5.3 fusion.15
  330.2 1.8 fusion.116
  335.0 6.3 fusion.22
  344.4 2.4 fusion.81
  346.9 4.4 collective-permute-start.4
  351.3 11.8 %collective-permute-start.5 = (f32[2,2,1,512,128]{3,2,4,1,0:T(1,128)}, f32[2,2,1,512,128]{3,2,4,1,0:T(1,128)S(1)}, u32[]{:S(2)}, u32[]{:S(2)}) collective-permute-start(f32[2,2,1,512,128]{3,2,4,1,0:T(1,128)} %get-tuple-element.79), channel_id=1, source_target_pairs={{1,0},{2,1},{3,2},{4,3},{5,4},{6,5},{7,6},{8,7},{9,8},{10,9},{11,1... | collective-permute-start | bytes 3145736 | tf_op jit(solution)/shard_map/ppermute | solution.py:30
  363.2 2.6 fusion.114
  368.1 21.7 %collective-permute-done.4 = f32[2,2,1,512,128]{3,2,4,1,0:T(1,128)S(1)} collective-permute-done((f32[2,2,1,512,128]{3,2,4,1,0:T(1,128)S(1)}, f32[2,2,1,512,128]{3,2,4,1,0:T(1,128)S(1)}, u32[]{:S(2)}, u32[]{:S(2)}) %collective-permute-start.4) | collective-permute-done | bytes 1048608 | tf_op jit(solution)/shard_map/ppermute | solution.py:27
  392.0 5.0 fusion.28
  397.0 1.8 fusion.108
  401.8 6.3 fusion.35
  411.2 2.4 fusion.80
  413.7 4.4 collective-permute-start.6
  418.1 1.7 collective-permute-start.7
  419.8 2.6 fusion.106
  424.7 35.4 %collective-permute-done.6 = f32[2,2,1,512,128]{3,2,4,1,0:T(1,128)S(1)} collective-permute-done((f32[2,2,1,512,128]{3,2,4,1,0:T(1,128)}, f32[2,2,1,512,128]{3,2,4,1,0:T(1,128)S(1)}, u32[]{:S(2)}, u32[]{:S(2)}) %collective-permute-start.6) | collective-permute-done | bytes 1048608 | tf_op jit(solution)/shard_map/ppermute | solution.py:27
  462.4 5.0 fusion.41
  467.4 1.8 fusion.100
  472.2 6.3 fusion.48
  481.6 2.4 fusion.79
  484.0 4.3 collective-permute-start.8
  489.9 2.6 fusion.98
  494.8 34.5 %collective-permute-done.8 = f32[2,2,1,512,128]{3,2,4,1,0:T(1,128)S(1)} collective-permute-done((f32[2,2,1,512,128]{3,2,4,1,0:T(1,128)S(1)}, f32[2,2,1,512,128]{3,2,4,1,0:T(1,128)S(1)}, u32[]{:S(2)}, u32[]{:S(2)}) %collective-permute-start.8) | collective-permute-done | bytes 1048608 | tf_op jit(solution)/shard_map/ppermute | solution.py:27
  531.5 5.0 fusion.54
  538.9 6.1 fusion.61
  547.7 1.7 fusion.78
  549.4 4.5 collective-permute-start.10
  558.4 35.6 %collective-permute-done.10 = f32[2,2,1,512,128]{3,2,4,1,0:T(1,128)S(1)} collective-permute-done((f32[2,2,1,512,128]{3,2,4,1,0:T(1,128)S(1)}, f32[2,2,1,512,128]{3,2,4,1,0:T(1,128)S(1)}, u32[]{:S(2)}, u32[]{:S(2)}) %collective-permute-start.10) | collective-permute-done | bytes 1048608 | tf_op jit(solution)/shard_map/ppermute | solution.py:27
  595.4 1.5 slice_bitcast_fusion.6
  597.0 5.9 fusion.75
  602.9 2.9 copy.91
  605.8 71.4 %reshape.42 = f32[2,2,2,128,4,32,4]{6,5,4,3,2,1,0:T(8,128)} reshape(f32[2,4,512,128]{3,2,1,0:T(8,128)} %copy.91) | data formatting | bytes 4194304 | tf_op jit(solution)/shard_map/reshape | solution.py:103
  677.2 20.8 %reduce_sum.9 = f32[2,2,128,32]{3,2,1,0:T(8,128)S(1)} reduce(f32[2,2,2,128,4,32,4]{6,5,4,3,2,1,0:T(8,128)} %reshape.42, f32[]{:T(128)} %constant.14.clone.1), dimensions={2,4,6}, to_apply=%region_2.3 | reduce | flops 507904 | bytes 2162692 | tf_op jit(solution)/shard_map/reduce_sum | solution.py:103
  698.8 1.7 div.10
  700.6 3.2 fusion.87
  707.6 5.0 fusion.68
  712.6 3.1 pad_maximum_fusion
  715.7 5.3 copy.92
  721.0 143.9 %all-gather.5.cloned.1.call-done = f32[2,32,8192]{2,0,1:T(2,128)} async-done(((f32[2,1,8192]{2,0,1:T(2,128)}), f32[2,32,8192]{2,0,1:T(2,128)}) %all-gather.5.cloned.1.call-update) | async-done | bytes 2097168 | tf_op jit(solution)/shard_map/all_gather | solution.py:107
  864.9 3.4 fusion.76
  (170 shorter events, 70.3 us)
Async XLA Ops:
  8.0 238.7 %all-gather.3.cloned.1.call-start = ((), (), s32[]{:S(2)}) async-start(), calls=%async_computation | async-start | bytes 2162688 | tf_op jit(solution)/shard_map/all_gather | solution.py:66
  9.6 240.0 %all-reduce.51.cloned.1.call-start = ((), (), s32[]{:S(2)}) async-start(), calls=%async_computation.2 | async-start | bytes 8388608 | tf_op jit(solution)/shard_map/psum | solution.py:19
  16.4 7.5 copy-start.43
  16.4 9.2 %copy-start.42 = (f32[4,512,128]{2,1,0:T(8,128)S(1)}, f32[4,512,128]{2,1,0:T(8,128)}, u32[]{:S(2)}) copy-start(f32[4,512,128]{2,1,0:T(8,128)} %param.6) | copy-start | bytes 3145732
  16.4 848.5 %all-gather.5.cloned.1.call-start = ((), (), s32[]{:S(2)}) async-start(), calls=%async_computation.1 | async-start | bytes 2162688 | tf_op jit(solution)/shard_map/all_gather | solution.py:107
  17.0 46.8 %collective-permute-start.1 = (f32[2,2,1,512,128]{3,2,4,1,0:T(1,128)S(1)}, f32[2,2,1,512,128]{3,2,4,1,0:T(1,128)}, u32[]{:S(2)}, u32[]{:S(2)}) collective-permute-start(f32[2,2,1,512,128]{3,2,4,1,0:T(1,128)S(1)} %broadcast.158), channel_id=1, source_target_pairs={{1,0},{2,1},{3,2},{4,3},{5,4},{6,5},{7,6},{8,7},{9,8},{10,9},{11,1... | collective-permute-start | bytes 3145736 | tf_op jit(solution)/shard_map/ppermute | solution.py:30
  18.3 73.7 %collective-permute-start = (f32[2,2,1,512,128]{3,2,4,1,0:T(1,128)S(1)}, f32[2,2,1,512,128]{3,2,4,1,0:T(1,128)}, u32[]{:S(2)}, u32[]{:S(2)}) collective-permute-start(f32[2,2,1,512,128]{3,2,4,1,0:T(1,128)S(1)} %broadcast.158), channel_id=1, source_target_pairs={{0,1},{1,2},{2,3},{3,4},{4,5},{5,6},{6,7},{7,8},{8,9},{9,10},{10,1... | collective-permute-start | bytes 3145736 | tf_op jit(solution)/shard_map/ppermute | solution.py:27
  249.6 3.2 copy-start.21
  249.6 3.2 copy-start.35
  254.8 5.4 copy-start.28
  257.5 4.1 copy-start.27
  262.9 2.1 copy-start.26
  262.9 2.1 copy-start.30
  263.0 2.2 copy-start.32
  263.0 2.2 copy-start.33
  264.5 1.3 copy-start.12
  264.5 1.6 copy-start.14
  264.5 1.9 copy-start.25
  264.5 2.0 copy-start.29
  271.4 6.8 copy-start.4
  271.4 22.8 %copy-start.6 = (f32[2,4,512,128]{2,1,3,0:T(4,128)}, f32[2,4,512,128]{2,1,3,0:T(4,128)S(1)}, u32[]{:S(2)}) copy-start(f32[2,4,512,128]{2,1,3,0:T(4,128)S(1)} %get-tuple-element.11) | copy-start | bytes 6291460
  286.4 33.8 %collective-permute-start.2 = (f32[2,2,1,512,128]{3,2,4,1,0:T(1,128)}, f32[2,2,1,512,128]{3,2,4,1,0:T(1,128)}, u32[]{:S(2)}, u32[]{:S(2)}) collective-permute-start(f32[2,2,1,512,128]{3,2,4,1,0:T(1,128)} %get-tuple-element.96), channel_id=1, source_target_pairs={{0,1},{1,2},{2,3},{3,4},{4,5},{5,6},{6,7},{7,8},{8,9},{9,10},{10,1... | collective-permute-start | bytes 3145736 | tf_op jit(solution)/shard_map/ppermute | solution.py:27
  292.7 29.4 %collective-permute-start.3 = (f32[2,2,1,512,128]{3,2,4,1,0:T(1,128)}, f32[2,2,1,512,128]{3,2,4,1,0:T(1,128)}, u32[]{:S(2)}, u32[]{:S(2)}) collective-permute-start(f32[2,2,1,512,128]{3,2,4,1,0:T(1,128)} %get-tuple-element.97), channel_id=1, source_target_pairs={{1,0},{2,1},{3,2},{4,3},{5,4},{6,5},{7,6},{8,7},{9,8},{10,9},{11,1... | collective-permute-start | bytes 3145736 | tf_op jit(solution)/shard_map/ppermute | solution.py:30
  302.1 3.8 copy-start.7
  302.1 22.7 %copy-start.22 = (f32[2,4,512,127]{2,1,3,0:T(4,128)S(1)}, f32[2,4,512,127]{2,1,3,0:T(4,128)}, u32[]{:S(2)}) copy-start(f32[2,4,512,127]{2,1,3,0:T(4,128)} %get-tuple-element.86) | copy-start | bytes 6242308
  302.1 22.7 %copy-start.23 = (f32[2,4,512,127]{2,1,3,0:T(4,128)S(1)}, f32[2,4,512,127]{2,1,3,0:T(4,128)}, u32[]{:S(2)}) copy-start(f32[2,4,512,127]{2,1,3,0:T(4,128)} %get-tuple-element.87) | copy-start | bytes 6242308
  305.9 18.9 %copy-start.17 = (f32[2,4,511,128]{2,1,3,0:T(4,128)S(1)}, f32[2,4,511,128]{2,1,3,0:T(4,128)}, u32[]{:S(2)}) copy-start(f32[2,4,511,128]{2,1,3,0:T(4,128)} %get-tuple-element.84) | copy-start | bytes 6279172
  305.9 18.9 %copy-start.18 = (f32[2,4,511,128]{2,1,3,0:T(4,128)S(1)}, f32[2,4,511,128]{2,1,3,0:T(4,128)}, u32[]{:S(2)}) copy-start(f32[2,4,511,128]{2,1,3,0:T(4,128)} %get-tuple-element.85) | copy-start | bytes 6279172
  305.9 18.9 %copy-start.19 = (f32[2,3,512,128]{2,1,3,0:T(4,128)S(1)}, f32[2,3,512,128]{2,1,3,0:T(4,128)}, u32[]{:S(2)}) copy-start(f32[2,3,512,128]{2,1,3,0:T(4,128)} %get-tuple-element.88) | copy-start | bytes 4718596
  306.0 18.9 %copy-start.20 = (f32[2,3,512,128]{2,1,3,0:T(4,128)S(1)}, f32[2,3,512,128]{2,1,3,0:T(4,128)}, u32[]{:S(2)}) copy-start(f32[2,3,512,128]{2,1,3,0:T(4,128)} %get-tuple-element.89) | copy-start | bytes 4718596
  306.8 18.1 %copy-start.5 = (f32[2,4,512,128]{2,1,3,0:T(4,128)S(1)}, f32[2,4,512,128]{2,1,3,0:T(4,128)}, u32[]{:S(2)}) copy-start(f32[2,4,512,128]{2,1,3,0:T(4,128)} %copy-done.4) | copy-start | bytes 6291460
  306.8 18.1 %copy-start.13 = (f32[4,512,128]{1,0,2:T(4,128)S(1)}, f32[4,512,128]{1,0,2:T(4,128)}, u32[]{:S(2)}) copy-start(f32[4,512,128]{1,0,2:T(4,128)} %copy.86) | copy-start | bytes 3145732
  306.8 18.1 %copy-start.15 = (f32[4,512,128]{1,0,2:T(4,128)S(1)}, f32[4,512,128]{1,0,2:T(4,128)}, u32[]{:S(2)}) copy-start(f32[4,512,128]{1,0,2:T(4,128)} %copy.85) | copy-start | bytes 3145732
  341.3 1.0 copy-start.38
  341.3 1.2 copy-start.39
  346.9 42.9 %collective-permute-start.4 = (f32[2,2,1,512,128]{3,2,4,1,0:T(1,128)S(1)}, f32[2,2,1,512,128]{3,2,4,1,0:T(1,128)S(1)}, u32[]{:S(2)}, u32[]{:S(2)}) collective-permute-start(f32[2,2,1,512,128]{3,2,4,1,0:T(1,128)S(1)} %get-tuple-element.78), channel_id=1, source_target_pairs={{0,1},{1,2},{2,3},{3,4},{4,5},{5,6},{6,7},{7,8},{8,9},{9,10},{10,1... | collective-permute-start | bytes 3145736 | tf_op jit(solution)/shard_map/ppermute | solution.py:27
  351.3 39.2 %collective-permute-start.5 = (f32[2,2,1,512,128]{3,2,4,1,0:T(1,128)}, f32[2,2,1,512,128]{3,2,4,1,0:T(1,128)S(1)}, u32[]{:S(2)}, u32[]{:S(2)}) collective-permute-start(f32[2,2,1,512,128]{3,2,4,1,0:T(1,128)} %get-tuple-element.79), channel_id=1, source_target_pairs={{1,0},{2,1},{3,2},{4,3},{5,4},{6,5},{7,6},{8,7},{9,8},{10,9},{11,1... | collective-permute-start | bytes 3145736 | tf_op jit(solution)/shard_map/ppermute | solution.py:30
  408.1 1.0 copy-start.36
  408.1 1.2 copy-start.37
  413.7 46.5 %collective-permute-start.6 = (f32[2,2,1,512,128]{3,2,4,1,0:T(1,128)}, f32[2,2,1,512,128]{3,2,4,1,0:T(1,128)S(1)}, u32[]{:S(2)}, u32[]{:S(2)}) collective-permute-start(f32[2,2,1,512,128]{3,2,4,1,0:T(1,128)} %get-tuple-element.60), channel_id=1, source_target_pairs={{0,1},{1,2},{2,3},{3,4},{4,5},{5,6},{6,7},{7,8},{8,9},{9,10},{10,1... | collective-permute-start | bytes 3145736 | tf_op jit(solution)/shard_map/ppermute | solution.py:27
  418.1 42.8 %collective-permute-start.7 = (f32[2,2,1,512,128]{3,2,4,1,0:T(1,128)S(1)}, f32[2,2,1,512,128]{3,2,4,1,0:T(1,128)S(1)}, u32[]{:S(2)}, u32[]{:S(2)}) collective-permute-start(f32[2,2,1,512,128]{3,2,4,1,0:T(1,128)S(1)} %get-tuple-element.61), channel_id=1, source_target_pairs={{1,0},{2,1},{3,2},{4,3},{5,4},{6,5},{7,6},{8,7},{9,8},{10,9},{11,1... | collective-permute-start | bytes 3145736 | tf_op jit(solution)/shard_map/ppermute | solution.py:30
  424.7 37.7 %copy-start.8 = (f32[4,512,128]{1,0,2:T(4,128)S(1)}, f32[4,512,128]{1,0,2:T(4,128)}, u32[]{:S(2)}) copy-start(f32[4,512,128]{1,0,2:T(4,128)} %copy.89) | copy-start | bytes 3145732
  424.7 37.7 %copy-start.10 = (f32[4,512,128]{1,0,2:T(4,128)S(1)}, f32[4,512,128]{1,0,2:T(4,128)}, u32[]{:S(2)}) copy-start(f32[4,512,128]{1,0,2:T(4,128)} %copy.90) | copy-start | bytes 3145732
  478.5 1.0 copy-start.40
  478.5 1.2 copy-start.41
  484.0 45.2 %collective-permute-start.8 = (f32[2,2,1,512,128]{3,2,4,1,0:T(1,128)S(1)}, f32[2,2,1,512,128]{3,2,4,1,0:T(1,128)S(1)}, u32[]{:S(2)}, u32[]{:S(2)}) collective-permute-start(f32[2,2,1,512,128]{3,2,4,1,0:T(1,128)S(1)} %get-tuple-element.40), channel_id=1, source_target_pairs={{0,1},{1,2},{2,3},{3,4},{4,5},{5,6},{6,7},{7,8},{8,9},{9,10},{10,1... | collective-permute-start | bytes 3145736 | tf_op jit(solution)/shard_map/ppermute | solution.py:27
  488.4 41.6 %collective-permute-start.9 = (f32[2,2,1,512,128]{3,2,4,1,0:T(1,128)}, f32[2,2,1,512,128]{3,2,4,1,0:T(1,128)S(1)}, u32[]{:S(2)}, u32[]{:S(2)}) collective-permute-start(f32[2,2,1,512,128]{3,2,4,1,0:T(1,128)} %get-tuple-element.41), channel_id=1, source_target_pairs={{1,0},{2,1},{3,2},{4,3},{5,4},{6,5},{7,6},{8,7},{9,8},{10,9},{11,1... | collective-permute-start | bytes 3145736 | tf_op jit(solution)/shard_map/ppermute | solution.py:30
  536.5 60.5 %copy-start = (f32[2,4,512,128]{2,1,3,0:T(4,128)}, f32[2,4,512,128]{2,1,3,0:T(4,128)S(1)}, u32[]{:S(2)}) copy-start(f32[2,4,512,128]{2,1,3,0:T(4,128)S(1)} %fusion.54) | copy-start | bytes 6291460
  536.5 2.3 copy-start.24
  545.0 52.0 %copy-start.2 = (f32[2,4,512,128]{2,1,3,0:T(4,128)}, f32[2,4,512,128]{2,1,3,0:T(4,128)S(1)}, u32[]{:S(2)}) copy-start(f32[2,4,512,128]{2,1,3,0:T(4,128)S(1)} %fusion.61) | copy-start | bytes 6291460
  549.4 44.5 %collective-permute-start.10 = (f32[2,2,1,512,128]{3,2,4,1,0:T(1,128)S(1)}, f32[2,2,1,512,128]{3,2,4,1,0:T(1,128)S(1)}, u32[]{:S(2)}, u32[]{:S(2)}) collective-permute-start(f32[2,2,1,512,128]{3,2,4,1,0:T(1,128)S(1)} %get-tuple-element.22), channel_id=1, source_target_pairs={{0,1},{1,2},{2,3},{3,4},{4,5},{5,6},{6,7},{7,8},{8,9},{9,10},{10,1... | collective-permute-start | bytes 3145736 | tf_op jit(solution)/shard_map/ppermute | solution.py:27
  553.9 41.6 %collective-permute-start.11 = (f32[2,2,1,512,128]{3,2,4,1,0:T(1,128)S(1)}, f32[2,2,1,512,128]{3,2,4,1,0:T(1,128)S(1)}, u32[]{:S(2)}, u32[]{:S(2)}) collective-permute-start(f32[2,2,1,512,128]{3,2,4,1,0:T(1,128)S(1)} %get-tuple-element.23), channel_id=1, source_target_pairs={{1,0},{2,1},{3,2},{4,3},{5,4},{6,5},{7,6},{8,7},{9,8},{10,9},{11,1... | collective-permute-start | bytes 3145736 | tf_op jit(solution)/shard_map/ppermute | solution.py:30
  700.6 3.2 copy-start.1
  705.2 1.6 copy-start.3
  705.2 1.8 copy-start.9
  705.2 2.2 copy-start.11
  705.2 2.3 copy-start.31
  705.2 2.4 copy-start.34
  707.6 5.0 copy-start.16
  715.7 149.2 %copy-start.44 = (s32[32]{0:T(128)S(1)}, s32[32]{0:T(128)}, u32[]{:S(2)}) copy-start(s32[32]{0:T(128)} %param.9) | copy-start | bytes 388
Sparse Core Ops, SparseCore 0:
  11.0 235.6 all-gather.2
  700.7 164.2 all-gather.4
Sparse Core Ops, SparseCore 1:
  16.5 147.6 all-reduce.50
where the time goes:
time: 884 us; the launch traced here: 877 us
  waiting for transfers between devices  499 us (56%)
  local copies, waits for them, and re-layouts  191 us (22%)
  other arithmetic  115 us (13%)
  starting transfers between devices  48.9 us (6%)
  between operations  19.7 us (2%)
    ppermute x6, waiting for transfers between devices, padded(): lax.ppermute(lax.slice_in_dim(block, block.shape[dim] - width, None, axis...  166 us
    all_gather x1, waiting for transfers between devices, local(): every = lax.all_gather(directions, 'space', axis=1, tiled=True)  152 us
    all_gather x1, waiting for transfers between devices, local(): gathered = lax.all_gather(coarse_q, 'space', axis=1, tiled=True)  144 us
    reshape x1, local copies, waits for them, and re-layouts, local(): second.reshape(dirs_dev, width_x // 2, 2, width_y // 4, 4, width_z // 4, 4)  71.4 us
    ppermute x6, waiting for transfers between devices, padded(): lax.ppermute(lax.slice_in_dim(block, 0, width, axis=dim), axis, backward)  37.1 us
    sub x5, other arithmetic, advance(): second + spread_b * lap_second - drift * (second - second_lower) + source  30.9 us
    ppermute x6, starting transfers between devices, padded(): lax.ppermute(lax.slice_in_dim(block, block.shape[dim] - width, None, axis...  29.5 us
    sub x5, other arithmetic, advance(): first + spread_a * lap_first - drift * (first - first_lower) - source  25.1 us
  transfers between devices with their start and end apart: 15, of which 9 were waited for; matrix products, arithmetic and copies ran while one was open for 8% of the time, Pallas kernels for 0%

commit v1 on v0

v1 whole, which is shorter than its diff:
```python
import jax
import jax.numpy as jnp
from jax import lax
from jax.experimental import pallas as pl
from jax.experimental.pallas import tpu as pltpu
from jax.sharding import PartitionSpec as P

N_SPACE = 32
NX = 128
ROWS = 264
PADR = 280
RC = 24
ORDER = (0, 3, 1, 2)
HI = lax.Precision.HIGHEST
F32 = jnp.float32


def remote(src, dst, send, recv, device):
    return pltpu.make_async_remote_copy(
        src_ref=src,
        dst_ref=dst,
        send_sem=send,
        recv_sem=recv,
        device_id=device,
        device_id_type=pl.DeviceIdType.MESH,
    )


def iota(shape, dim):
    return lax.broadcasted_iota(jnp.int32, shape, dim)


def sweep(
    owner, block, store, rate, dirs, out, sens,
    slab, cand0, cand1, ring0, ring1, ext0, ext1, rext, coef, vfine, state,
    got1, put2, got2, coarse, wide, umat, inverse, means, got3, put3,
    lsem, slab_s, slab_r, rz_s, rz_r, rx_s, rx_r,
    z0_s, z0_r, f0_s, f0_r, x0_s, x0_r, g_s, g_r,
    z1_s, z1_r, f1_s, f1_r, x1_s, x1_r,
    d1_s, d1_r, d2_s, d2_r, d3_s, d3_r, n1_s, n1_r, n1_x, n2_s, n2_r, o_s, o_r, o_l,
):
    me = lax.axis_index("space")
    di = lax.axis_index("dir")
    core = di % 2
    zh = di // 2
    zl = me % 2
    col = me // 2
    z = zh * 2 + zl
    up = (z + 1) % 4
    down = (z + 3) % 4
    zp = ((up // 2) * 2 + core, col * 2 + up % 2)
    zm = ((down // 2) * 2 + core, col * 2 + down % 2)
    mate = (zh * 2 + 1 - core, me)
    xr = (di, ((col + 1) % 16) * 2 + zl)
    xl = (di, ((col + 15) % 16) * 2 + zl)
    xt = (di, ((col + 1 + 14 * zl) % 16) * 2 + zl)
    near = 9 - 8 * zl
    far = 1 + 8 * zl
    own0 = jnp.where(owner[0] // 2 == zh, 1, 0)
    own1 = jnp.where(owner[1] // 2 == zh, 1, 0)
    core0 = owner[0] % 2
    core1 = owner[1] % 2

    barrier = pltpu.get_barrier_semaphore()

    @pl.loop(1, N_SPACE)
    def _(r):
        pl.semaphore_signal(
            barrier, inc=1, device_id=(di, (me + r) % N_SPACE), device_id_type=pl.DeviceIdType.MESH
        )

    @pl.loop(0, N_SPACE)
    def _(r):
        pl.semaphore_signal(
            barrier,
            inc=1,
            device_id=(zh * 2 + 1 - core, (me + r) % N_SPACE),
            device_id_type=pl.DeviceIdType.MESH,
        )

    other = ((1 - zh) * 2 + core, col * 2 + 1 - zl)
    pl.semaphore_signal(barrier, inc=1, device_id=other, device_id_type=pl.DeviceIdType.MESH)

    mine = pl.ds(248 * core, ROWS)
    theirs = pl.ds(248 * (1 - core), ROWS)
    local_slab = pltpu.make_async_copy(store.at[0, :, :, mine], slab.at[core], lsem.at[0])
    local_rate = pltpu.make_async_copy(rate.at[:, mine], rext.at[0], lsem.at[1])
    local_slab.start()
    local_rate.start()
    pl.semaphore_wait(barrier, 64)

    slab_copy = remote(store.at[0, :, :, theirs], slab.at[core], slab_s, slab_r, mate)
    slab_copy.start()

    @pl.loop(1, N_SPACE)
    def _(r):
        to = (me + r) % N_SPACE
        remote(dirs.at[:, to], got1.at[me], d1_s, d1_r, (di, to)).start()

    d1_local = pltpu.make_async_copy(dirs.at[:, me], got1.at[me], lsem.at[2])
    d1_local.start()

    rate_up = remote(rate.at[pl.ds(0, 2), mine], rext.at[1, pl.ds(0, 2)], rz_s.at[0], rz_r.at[0], zp)
    rate_down = remote(rate.at[pl.ds(2, 2), mine], rext.at[1, pl.ds(2, 2)], rz_s.at[1], rz_r.at[1], zm)
    rate_up.start()
    rate_down.start()

    @pl.loop(0, 14)
    def _(i):
        for d in range(4):
            for sp in range(2):
                for b in range(2):
                    state[b, d, sp, i] = jnp.zeros((PADR, 128), F32)

    local_slab.wait()
    slab_copy.wait_recv()

    def choose(cand, which):
        @pl.loop(0, 4)
        def _(i):
            for sp in range(2):
                first = jnp.broadcast_to(which == 0, (ROWS, 128))
                cand[sp, i] = jnp.where(first, slab[0, sp, i], slab[1, sp, i])

    def ring_copies(cand, ring, s, r):
        copies = []
        for i in ORDER:
            copies.append(remote(cand.at[:, i], ring.at[0, :, i], s.at[0, i], r.at[0, i], zp))
            copies.append(remote(cand.at[:, i], ring.at[1, :, i], s.at[1, i], r.at[1, i], zm))
        return copies

    choose(cand0, core0)
    ring_a = ring_copies(cand0, ring0, z0_s, z0_r)
    for copy in ring_a:
        copy.start()
    choose(cand1, core1)

    d1_local.wait()
    piece31 = got1.at[pl.ds(0, N_SPACE - 1)]
    remote(piece31, piece31, d1_s, d1_r, mate).wait_recv()
    late = jnp.where(me >= 16, 1, 0)

    @pl.loop(0, N_SPACE)
    def _(r):
        to = (me + r) % N_SPACE
        for e in range(4):
            at = jnp.clip(to + (e - 1) - late, 0, N_SPACE - 1)
            put2[r, e] = got1[block[at]]

    @pl.loop(1, N_SPACE)
    def _(r):
        to = (me + r) % N_SPACE
        remote(put2.at[r], got2.at[me], d2_s, d2_r, (di, to)).start()

    d2_local = pltpu.make_async_copy(put2.at[0], got2.at[me], lsem.at[3])
    d2_local.start()

    rate_x = []
    for h, copy in enumerate((rate_up, rate_down)):
        copy.wait_recv()
        part = pl.ds(2 * h, 2)
        rate_x.append(remote(rext.at[1, part], rext.at[2, part], rx_s.at[h], rx_r.at[h], xt))
        rate_x[-1].start()

    def ring_step(t, cand, ring, own, ext, z_r, f_s, f_r):
        forwards = []
        same = jnp.where(zl == 0, own, 1 - own)
        for i in ORDER:
            remote(cand.at[:, i], ring.at[0, :, i], f_s.at[i], z_r.at[0, i], zp).wait_recv()
            remote(cand.at[:, i], ring.at[1, :, i], f_s.at[i], z_r.at[1, i], zm).wait_recv()
            src, to = (0, zp) if i < 2 else (1, zm)
            copy = remote(ring.at[src, :, i], ring.at[2, :, i], f_s.at[i], f_r.at[i], to)
            copy.start()
            forwards.append(copy)
            for sp in range(2):
                from_up = jnp.broadcast_to(same == 1, (ROWS, 128))
                ext[0, sp, i] = jnp.where(from_up, ring[1, sp, i], ring[0, sp, i])
            if t == 0:
                copy = remote(ext.at[0, :, i], ext.at[1, :, i], x0_s.at[i], x0_r.at[i], xt)
                copy.start()
                forwards.append(copy)
        return forwards

    sent_a = ring_step(0, cand0, ring0, own0, ext0, z0_r, f0_s, f0_r)
    ring_b = ring_copies(cand1, ring1, z1_s, z1_r)
    for copy in ring_b:
        copy.start()

    @pl.loop(0, N_SPACE)
    def _(b):
        at = jnp.int32(0)
        for s in range(N_SPACE):
            at = jnp.where(block[s] == b, s, at)
        inverse[b] = at

    row = iota((ROWS, 128), 0) + 248 * core
    lane = iota((ROWS, 128), 1)
    cy = row >> 2
    umat[...] = jnp.where(((cy & 3) == (lane >> 5)) & ((cy >> 2) == (lane & 31)), 1.0, 0.0)

    d2_local.wait()
    piece31 = got2.at[pl.ds(0, N_SPACE - 1)]
    remote(piece31, piece31, d2_s, d2_r, mate).wait_recv()

    @pl.loop(0, 2)
    def _(d):
        for k in range(8):
            for jj in range(16):
                coarse[2 * core + d, k, 2 * jj : 2 * jj + 2] = got2[16 * (1 - k % 2) + jj, k // 2, d]

    coarse_mine = coarse.at[pl.ds(2 * core, 2)]
    coarse_copy = remote(coarse_mine, coarse_mine, d3_s, d3_r, mate)
    coarse_copy.start()
    coarse_copy.wait_recv()

    k_in = iota((128, 128), 0)
    k_out = iota((128, 128), 1)

    @pl.loop(0, 32)
    def _(n):
        d = n // 8
        k = n % 8
        block_c = coarse[d, k]
        for jj in range(4):
            w = jnp.where(k_in == 32 * jj + (k_out >> 2), 1.0, 0.0).astype(F32)
            wide[32 * jj : 32 * jj + 32] = jnp.dot(block_c, w, precision=HI, preferred_element_type=F32)
        vfine[d, k] = jnp.dot(umat[...], wide[...], precision=HI, preferred_element_type=F32)

    def put_coef(at, a, b, r):
        ra = 0.1 * r * a
        coef[0, at] = ra
        coef[1, at] = 0.1 * r * b
        coef[2, at] = ra * b

    def own_coef(cand, ring, own, i):
        here = jnp.broadcast_to(own == 1, (ROWS, 128))
        a = jnp.where(here, cand[0, i], ring[2, 0, i])
        b = jnp.where(here, cand[1, i], ring[2, 1, i])
        put_coef(5 + i, a, b, rext[0, i])

    local_rate.wait()
    for i in ORDER:
        remote(cand0.at[:, i], ring0.at[2, :, i], f0_s.at[i], f0_r.at[i], zp).wait_recv()
        own_coef(cand0, ring0, own0, i)
    edge_r = remote(coef.at[2, 8], coef.at[2, 0], g_s.at[0], g_r.at[0], xr)
    edge_l = remote(coef.at[2, 5], coef.at[2, 13], g_s.at[1], g_r.at[1], xl)
    edge_r.start()
    edge_l.start()

    @pl.loop(0, 4)
    def _(i):
        put_coef(near + i, ext0[0, 0, i], ext0[0, 1, i], rext[1, i])

    for copy in rate_x:
        copy.wait_recv()
    for i in ORDER:
        remote(ext0.at[0, :, i], ext0.at[1, :, i], x0_s.at[i], x0_r.at[i], xt).wait_recv()
        put_coef(far + i, ext0[1, 0, i], ext0[1, 1, i], rext[2, i])
    edge_r.wait_recv()
    edge_l.wait_recv()

    low = 5 - 4 * me
    high = NX + 5 - 4 * me

    @pl.loop(jnp.maximum(0, low), jnp.minimum(14, high))
    def _(i):
        k = (i + 1) // 2
        for d in range(4):
            src = vfine[d, k] * coef[2, i]
            state[0, d, 0, i, 8 : 8 + ROWS] = -src
            state[0, d, 1, i, 8 : 8 + ROWS] = src

    lanes = iota((RC, 128), 1)
    first_lane = lanes == 0
    last_lane = lanes == 127

    def plane(b, i):
        k = (i + 1) // 2

        @pl.loop(0, ROWS // RC)
        def _(n):
            at = pl.multiple_of(n * RC, 8)
            rows = pl.ds(at, RC)
            ra = coef[0, i, rows]
            rb = coef[1, i, rows]
            g = coef[2, i, rows]
            for d in range(4):
                def around(sp):
                    x = state[b, d, sp, i, pl.ds(at + 8, RC)]
                    low_x = state[b, d, sp, i - 1, pl.ds(at + 8, RC)]
                    s = state[b, d, sp, i + 1, pl.ds(at + 8, RC)]
                    s = s + state[b, d, sp, i, pl.ds(at + 7, RC)]
                    s = s + state[b, d, sp, i, pl.ds(at + 9, RC)]
                    s = s + jnp.where(first_lane, 0.0, pltpu.roll(x, 1, 1))
                    s = s + jnp.where(last_lane, 0.0, pltpu.roll(x, 127, 1))
                    return x, low_x, s

                p, p_low, p_sum = around(0)
                q, q_low, q_sum = around(1)
                src = vfine[d, k, rows] * g + p * rb + q * ra
                state[1 - b, d, 0, i, pl.ds(at + 8, RC)] = (
                    0.27 * p + 0.08 * p_sum + 0.33 * p_low - src
                )
                state[1 - b, d, 1, i, pl.ds(at + 8, RC)] = (
                    0.34 * q + 0.06 * q_sum + 0.31 * q_low + src
                )

    def update(u):
        @pl.loop(jnp.maximum(u - 1, low), jnp.minimum(15 - u, high))
        def _(i):
            plane(u % 2, i)

    update(2)
    update(3)

    sent_b = ring_step(1, cand1, ring1, own1, ext1, z1_r, f1_s, f1_r)
    part = pl.ds(2 - 2 * zl, 2)
    x1 = remote(ext1.at[0, :, part], ext1.at[1, :, part], x1_s, x1_r, xt)
    x1.start()
    edge_r.wait_send()
    edge_l.wait_send()
    for i in ORDER:
        remote(cand1.at[:, i], ring1.at[2, :, i], f1_s.at[i], f1_r.at[i], zp).wait_recv()
        own_coef(cand1, ring1, own1, i)
    x1.wait_recv()

    @pl.loop(0, 2)
    def _(i):
        n = i + 2 * zl
        put_coef(near + n, ext1[0, 0, n], ext1[0, 1, n], rext[1, n])
        m = i + 2 - 2 * zl
        put_coef(far + m, ext1[1, 0, m], ext1[1, 1, m], rext[2, m])

    update(4)
    update(5)

    half = pl.ds(256 * core, 256)
    held = pl.ds(8 + 8 * core, 256)

    def out_copies(i):
        here = pltpu.make_async_copy(
            state.at[1, pl.ds(2 * core, 2), :, 5 + i, held],
            out.at[:, :, i, half],
            o_l.at[i],
        )
        there = remote(
            state.at[1, pl.ds(2 - 2 * core, 2), :, 5 + i, held],
            out.at[:, :, i, half],
            o_s.at[i],
            o_r.at[i],
            mate,
        )
        return here, there

    srow = iota((64, 256), 0)
    scol = iota((64, 256), 1) >> 2

    @pl.loop(0, 4)
    def _(i):
        plane(0, 5 + i)
        here, there = out_copies(i)
        here.start()
        there.start()

    smat = jnp.where(scol == 4 * (srow & 15) + (srow >> 4), 1.0 / 32.0, 0.0).astype(F32)

    @pl.loop(0, 8)
    def _(n):
        cp = n // 4
        d = n % 4
        q = state[1, d, 1, 5 + 2 * cp, held] + state[1, d, 1, 6 + 2 * cp, held]
        m = jnp.dot(smat, q, precision=HI, preferred_element_type=F32)
        acc = jnp.zeros((16, 128), F32)
        for jj in range(4):
            t = jnp.where(k_out == 32 * jj + (k_in >> 2), 1.0, 0.0).astype(F32)
            acc = acc + jnp.dot(m[16 * jj : 16 * jj + 16], t, precision=HI, preferred_element_type=F32)
        for g in range(4):
            means[d // 2, (d % 2) * 8 + cp * 4 + g] = acc[4 * g : 4 * g + 4]

    self_piece = me // 16 == core

    @pl.loop(1, 16)
    def _(r):
        j = (me + r) % 16
        remote(means.at[core, j], got3.at[me], n1_s, n1_r, (di, 16 * core + j)).start()

    @pl.loop(0, 16)
    def _(r):
        j = (me + r) % 16
        remote(
            means.at[1 - core, j], got3.at[me], n1_s, n1_r, (zh * 2 + 1 - core, 16 * core + j)
        ).start()

    j0 = me % 16
    to_self = pltpu.make_async_copy(means.at[core, j0], got3.at[me], n1_r)
    to_twin = remote(means.at[core, j0], got3.at[me], n1_x, n1_r, (di, 16 * core + j0))

    @pl.when(self_piece)
    def _():
        to_self.start()

    @pl.when(jnp.logical_not(self_piece))
    def _():
        to_twin.start()

    remote(got3, got3, n1_s, n1_r, mate).wait_recv()

    @pl.loop(0, N_SPACE)
    def _(r):
        put3[r] = got3[inverse[(me + r) % N_SPACE]]

    cc = me // 16
    dl = (me // 8) % 2
    cp = (me // 4) % 2
    rg = me % 4

    @pl.loop(1, N_SPACE)
    def _(r):
        to = (me + r) % N_SPACE
        remote(put3.at[r], sens.at[dl, cp, cc, rg], n2_s, n2_r, (di, to)).start()

    sens_local = pltpu.make_async_copy(put3.at[0], sens.at[dl, cp, cc, rg], lsem.at[4])
    sens_local.start()

    sens_local.wait()
    piece31 = put3.at[pl.ds(0, N_SPACE - 1)]
    last = remote(piece31, piece31, n2_s, n2_r, mate)
    last.wait_send()
    last.wait_recv()
    remote(piece31, piece31, n1_s, n1_r, mate).wait_send()

    @pl.when(jnp.logical_not(self_piece))
    def _():
        to_twin.wait_send()

    for i in range(4):
        here, there = out_copies(i)
        here.wait()
        there.wait_send()
        there.wait_recv()
    piece31 = got1.at[pl.ds(0, N_SPACE - 1)]
    remote(piece31, piece31, d1_s, d1_r, mate).wait_send()
    piece31 = got2.at[pl.ds(0, N_SPACE - 1)]
    remote(piece31, piece31, d2_s, d2_r, mate).wait_send()
    coarse_copy.wait_send()
    slab_copy.wait_send()
    for copy in [rate_up, rate_down, x1] + rate_x + ring_a + ring_b + sent_a + sent_b:
        copy.wait_send()


def local(store, rate, directions, owner_map, block_map):
    dma = pltpu.SemaphoreType.DMA
    plane_pair = (2, 4, ROWS, 128)
    vmem = pltpu.VMEM
    scratch = [
        vmem((2,) + plane_pair, F32),
        vmem(plane_pair, F32),
        vmem(plane_pair, F32),
        vmem((3,) + plane_pair, F32),
        vmem((3,) + plane_pair, F32),
        vmem((2,) + plane_pair, F32),
        vmem((2,) + plane_pair, F32),
        vmem((3, 4, ROWS, 128), F32),
        vmem((3, 14, ROWS, 128), F32),
        vmem((4, 8, ROWS, 128), F32),
        vmem((2, 4, 2, 14, PADR, 128), F32),
        vmem((32, 2, 2, 128), F32),
        vmem((32, 4, 2, 2, 128), F32),
        vmem((32, 4, 2, 2, 128), F32),
        vmem((4, 8, 32, 128), F32),
        vmem((128, 128), F32),
        vmem((ROWS, 128), F32),
        pltpu.SMEM((32,), jnp.int32),
        vmem((2, 16, 4, 128), F32),
        vmem((32, 4, 128), F32),
        vmem((32, 4, 128), F32),
        dma((5,)), dma, dma, dma((2,)), dma((2,)), dma((2,)), dma((2,)),
        dma((2, 4)), dma((2, 4)), dma((4,)), dma((4,)), dma((4,)), dma((4,)), dma((2,)), dma((2,)),
        dma((2, 4)), dma((2, 4)), dma((4,)), dma((4,)), dma, dma,
        dma, dma, dma, dma, dma, dma, dma, dma, dma, dma, dma, dma((4,)), dma((4,)), dma((4,)),
    ]
    hbm = pl.BlockSpec(memory_space=pl.ANY)
    smem = pl.BlockSpec(memory_space=pltpu.SMEM)
    tangent, sens = pl.pallas_call(
        sweep,
        out_shape=(
            jax.ShapeDtypeStruct((2, 2, 4, 512, 128), F32),
            jax.ShapeDtypeStruct((2, 2, 2, 4, 4, 128), F32),
        ),
        in_specs=[smem, smem, hbm, hbm, hbm],
        out_specs=(hbm, hbm),
        scratch_shapes=scratch,
        compiler_params=pltpu.CompilerParams(
            collective_id=0, has_side_effects=True, vmem_limit_bytes=67043328
        ),
        name="sweep",
    )(owner_map, block_map, store, rate, directions.reshape(2, 32, 2, 128))
    return tangent, sens.reshape(2, 1, 8192)


def solution(mesh):
    return jax.shard_map(
        local,
        mesh=mesh,
        in_specs=(
            P("dir", None, "space", None, None),
            P("space", None, None),
            P("dir", "space", None),
            P(),
            P(),
        ),
        out_specs=(P("dir", None, "space", None, None), P("dir", "space", None)),
        check_vma=False,
    )
```

time: 884 us -> 168 us (0.19)
  waiting for transfers between devices: 499 us -> 0 us
  local copies, waits for them, and re-layouts: 191 us -> 5.27 us
  Pallas kernels: 0 us -> 162 us
  other arithmetic: 115 us -> 0 us
  starting transfers between devices: 48.9 us -> 0 us
  between operations: 19.7 us -> 0.65 us
    all_gather x2 -> x0, waiting for transfers between devices: 296 us -> none  [the longest x1 152 us: local(): every = lax.all_gather(directions, 'space', axis=1, tiled=True)]
    ppermute x12 -> x0, waiting for transfers between devices: 203 us -> none  [the longest x6 166 us: padded(): lax.ppermute(lax.slice_in_dim(block, block.shape[dim] - width, None, axis...]
    pallas_call x0 -> x1, Pallas kernels: none -> 162 us  [local(): pl.pallas_call(sweep, out_shape=(jax.ShapeDtypeStruct((2, 2, 4, 512, 128)...]
    reshape x1 -> x0, local copies, waits for them, and re-layouts: 71.4 us -> none  [local(): second.reshape(dirs_dev, width_x // 2, 2, width_y // 4, 4, width_z // 4, 4)]
    slice x41 -> x0, local copies, waits for them, and re-layouts: 60.2 us -> none  [the longest x10 19.2 us: across_yz(): total = total + jnp.pad(field[..., :, 1:], lead + ((0, 0), (0, 1)))]
    sub x10 -> x0, other arithmetic: 56 us -> none  [the longest x5 30.9 us: advance(): second + spread_b * lap_second - drift * (second - second_lower) + source]
    ppermute x12 -> x0, starting transfers between devices: 48.8 us -> none  [the longest x6 29.5 us: padded(): lax.ppermute(lax.slice_in_dim(block, block.shape[dim] - width, None, axis...]
    another operation x18 -> x0, other arithmetic: 32.4 us -> none  [the longest x15 21.1 us: local(): jnp.stack([jnp.concatenate([first[:, :1], first[:, -1:]], 1), jnp.concate...]
  transfers between devices with their start and end apart: 15 -> 0, of which waited for: 9 -> 0; matrix products, arithmetic and copies ran while one was open for 8% -> 0% of each run, Pallas kernels for 0% -> 0%
where the time goes in v1:
time: 168 us
  Pallas kernels  162 us (96%)
  local copies, waits for them, and re-layouts  5.27 us (3%)
    pallas_call x1, Pallas kernels, local(): pl.pallas_call(sweep, out_shape=(jax.ShapeDtypeStruct((2, 2, 4, 512, 128)...  162 us
    unnamed x4, local copies, waits for them, and re-layouts  5.27 us

profile of v1, /device:TPU:0, one launch (start us, length us, event | category | flops | bytes accessed | tf_op | source)
XLA Modules:
  0.0 167.8 jit_solution(7317097073303150615)
XLA Ops:
  0.6 161.9 %sweep.1 = (f32[2,2,4,512,128]{4,3,2,1,0:T(8,128)}, f32[2,2,2,4,4,128]{5,4,3,2,1,0:T(4,128)}) custom-call(s32[4]{0:T(128)} %owner.1, s32[32]{0:T(128)} %block.1, f32[1,2,4,512,128]{4,3,2,1,0:T(8,128)} %store.1, f32[4,512,128]{2,1,0:T(8,128)} %rate.1, f32[2,32,2,128]{3,2,1,0:T(2,128)} %bitcast.2), custom_call_target="tpu_custom_call" | custom-call | tf_op jit(solution)/shard_map/sweep/pallas_call | solution.py:484
  162.6 0.0 copy-start
  162.6 4.6 %copy.10 = f32[2,2,4,512,128]{4,3,2,1,0:T(8,128)} copy(f32[2,2,4,512,128]{4,3,2,1,0:T(8,128)} %get-tuple-element.10) | data formatting | bytes 8388608
  167.2 0.0 copy-done
  167.2 0.6 copy.11
Async XLA Ops:
  162.6 4.6 %copy-start = (f32[2,2,2,4,4,128]{5,4,3,2,1,0:T(4,128)S(1)}, f32[2,2,2,4,4,128]{5,4,3,2,1,0:T(4,128)}, u32[]{:S(2)}) copy-start(f32[2,2,2,4,4,128]{5,4,3,2,1,0:T(4,128)} %get-tuple-element.5) | copy-start | bytes 196612

commit v2 on v1

--- a/solution.py
+++ b/solution.py
@@ -10,9 +10,10 @@
 ROWS = 264
 PADR = 280
 RC = 24
+PARTS = 11
 ORDER = (0, 3, 1, 2)
-HI = lax.Precision.HIGHEST
 F32 = jnp.float32
+BF16 = jnp.bfloat16
 
 
 def remote(src, dst, send, recv, device):
@@ -26,6 +27,17 @@
     )
 
 
+def one_hot(where):
+    return jnp.where(where, 1.0, 0.0).astype(BF16)
+
+
+def thirds(x):
+    a = x.astype(BF16)
+    rest = x - a.astype(F32)
+    b = rest.astype(BF16)
+    return a, b, (rest - b.astype(F32)).astype(BF16)
+
+
 def iota(shape, dim):
     return lax.broadcasted_iota(jnp.int32, shape, dim)
 
@@ -33,7 +45,7 @@
 def sweep(
     owner, block, store, rate, dirs, out, sens,
     slab, cand0, cand1, ring0, ring1, ext0, ext1, rext, coef, vfine, state,
-    got1, put2, got2, coarse, wide, umat, inverse, means, got3, put3,
+    got1, put2, got2, coarse, wide, umat, wmat, tmat, smat, inverse, means, got3, put3,
     lsem, slab_s, slab_r, rz_s, rz_r, rx_s, rx_r,
     z0_s, z0_r, f0_s, f0_r, x0_s, x0_r, g_s, g_r,
     z1_s, z1_r, f1_s, f1_r, x1_s, x1_r,
@@ -87,24 +99,6 @@
     local_rate = pltpu.make_async_copy(rate.at[:, mine], rext.at[0], lsem.at[1])
     local_slab.start()
     local_rate.start()
-    pl.semaphore_wait(barrier, 64)
-
-    slab_copy = remote(store.at[0, :, :, theirs], slab.at[core], slab_s, slab_r, mate)
-    slab_copy.start()
-
-    @pl.loop(1, N_SPACE)
-    def _(r):
-        to = (me + r) % N_SPACE
-        remote(dirs.at[:, to], got1.at[me], d1_s, d1_r, (di, to)).start()
-
-    d1_local = pltpu.make_async_copy(dirs.at[:, me], got1.at[me], lsem.at[2])
-    d1_local.start()
-
-    rate_up = remote(rate.at[pl.ds(0, 2), mine], rext.at[1, pl.ds(0, 2)], rz_s.at[0], rz_r.at[0], zp)
-    rate_down = remote(rate.at[pl.ds(2, 2), mine], rext.at[1, pl.ds(2, 2)], rz_s.at[1], rz_r.at[1], zm)
-    rate_up.start()
-    rate_down.start()
-
     @pl.loop(0, 14)
     def _(i):
         for d in range(4):
@@ -112,6 +106,24 @@
                 for b in range(2):
                     state[b, d, sp, i] = jnp.zeros((PADR, 128), F32)
 
+    pl.semaphore_wait(barrier, 64)
+
+    slab_copy = remote(store.at[0, :, :, theirs], slab.at[core], slab_s, slab_r, mate)
+    slab_copy.start()
+
+    @pl.loop(1, N_SPACE)
+    def _(r):
+        to = (me + r) % N_SPACE
+        remote(dirs.at[:, to], got1.at[me], d1_s, d1_r, (di, to)).start()
+
+    d1_local = pltpu.make_async_copy(dirs.at[:, me], got1.at[me], lsem.at[2])
+    d1_local.start()
+
+    rate_up = remote(rate.at[pl.ds(0, 2), mine], rext.at[1, pl.ds(0, 2)], rz_s.at[0], rz_r.at[0], zp)
+    rate_down = remote(rate.at[pl.ds(2, 2), mine], rext.at[1, pl.ds(2, 2)], rz_s.at[1], rz_r.at[1], zm)
+    rate_up.start()
+    rate_down.start()
+
     local_slab.wait()
     slab_copy.wait_recv()
 
@@ -131,7 +143,7 @@
 
     choose(cand0, core0)
     ring_a = ring_copies(cand0, ring0, z0_s, z0_r)
-    for copy in ring_a:
+    for copy in ring_a[:2]:
         copy.start()
     choose(cand1, core1)
 
@@ -154,6 +166,9 @@
 
     d2_local = pltpu.make_async_copy(put2.at[0], got2.at[me], lsem.at[3])
     d2_local.start()
+
+    for copy in ring_a[2:]:
+        copy.start()
 
     rate_x = []
     for h, copy in enumerate((rate_up, rate_down)):
@@ -162,10 +177,10 @@
         rate_x.append(remote(rext.at[1, part], rext.at[2, part], rx_s.at[h], rx_r.at[h], xt))
         rate_x[-1].start()
 
-    def ring_step(t, cand, ring, own, ext, z_r, f_s, f_r):
+    def ring_step(t, cand, ring, own, ext, z_r, f_s, f_r, planes):
         forwards = []
         same = jnp.where(zl == 0, own, 1 - own)
-        for i in ORDER:
+        for i in planes:
             remote(cand.at[:, i], ring.at[0, :, i], f_s.at[i], z_r.at[0, i], zp).wait_recv()
             remote(cand.at[:, i], ring.at[1, :, i], f_s.at[i], z_r.at[1, i], zm).wait_recv()
             src, to = (0, zp) if i < 2 else (1, zm)
@@ -181,11 +196,6 @@
                 forwards.append(copy)
         return forwards
 
-    sent_a = ring_step(0, cand0, ring0, own0, ext0, z0_r, f0_s, f0_r)
-    ring_b = ring_copies(cand1, ring1, z1_s, z1_r)
-    for copy in ring_b:
-        copy.start()
-
     @pl.loop(0, N_SPACE)
     def _(b):
         at = jnp.int32(0)
@@ -196,7 +206,18 @@
     row = iota((ROWS, 128), 0) + 248 * core
     lane = iota((ROWS, 128), 1)
     cy = row >> 2
-    umat[...] = jnp.where(((cy & 3) == (lane >> 5)) & ((cy >> 2) == (lane & 31)), 1.0, 0.0)
+    umat[...] = one_hot(((cy & 3) == (lane >> 5)) & ((cy >> 2) == (lane & 31)))
+    k_in = iota((128, 128), 0)
+    k_out = iota((128, 128), 1)
+    for jj in range(4):
+        wmat[:, 128 * jj : 128 * jj + 128] = one_hot(k_in == 32 * jj + (k_out >> 2))
+        tmat[jj] = one_hot(k_out == 32 * jj + (k_in >> 2))
+    srow = iota((64, 256), 0)
+    scol = iota((64, 256), 1) >> 2
+    smat[...] = one_hot(scol == 4 * (srow & 15) + (srow >> 4))
+
+    args_a = (0, cand0, ring0, own0, ext0, z0_r, f0_s, f0_r)
+    sent_a = ring_step(*args_a, ORDER[:2])
 
     d2_local.wait()
     piece31 = got2.at[pl.ds(0, N_SPACE - 1)]
@@ -211,20 +232,27 @@
     coarse_mine = coarse.at[pl.ds(2 * core, 2)]
     coarse_copy = remote(coarse_mine, coarse_mine, d3_s, d3_r, mate)
     coarse_copy.start()
+
+    sent_a += ring_step(*args_a, ORDER[2:3])
     coarse_copy.wait_recv()
 
-    k_in = iota((128, 128), 0)
-    k_out = iota((128, 128), 1)
-
-    @pl.loop(0, 32)
-    def _(n):
+    def expand(n):
         d = n // 8
         k = n % 8
-        block_c = coarse[d, k]
-        for jj in range(4):
-            w = jnp.where(k_in == 32 * jj + (k_out >> 2), 1.0, 0.0).astype(F32)
-            wide[32 * jj : 32 * jj + 32] = jnp.dot(block_c, w, precision=HI, preferred_element_type=F32)
-        vfine[d, k] = jnp.dot(umat[...], wide[...], precision=HI, preferred_element_type=F32)
+        total = jnp.zeros((ROWS, 128), F32)
+        for h, part in enumerate(thirds(coarse[d, k])):
+            x = jnp.dot(part, wmat[...], preferred_element_type=F32).astype(BF16)
+            for jj in range(4):
+                wide[h, 32 * jj : 32 * jj + 32] = x[:, 128 * jj : 128 * jj + 128]
+            total = total + jnp.dot(umat[...], wide[h], preferred_element_type=F32)
+        vfine[d, k] = total
+
+    pl.loop(0, 16)(expand)
+    sent_a += ring_step(*args_a, ORDER[3:])
+    ring_b = ring_copies(cand1, ring1, z1_s, z1_r)
+    for copy in ring_b:
+        copy.start()
+    pl.loop(16, 32)(expand)
 
     def put_coef(at, a, b, r):
         ra = 0.1 * r * a
@@ -274,46 +302,50 @@
     first_lane = lanes == 0
     last_lane = lanes == 127
 
-    def plane(b, i):
-        k = (i + 1) // 2
-
-        @pl.loop(0, ROWS // RC)
-        def _(n):
-            at = pl.multiple_of(n * RC, 8)
-            rows = pl.ds(at, RC)
-            ra = coef[0, i, rows]
-            rb = coef[1, i, rows]
-            g = coef[2, i, rows]
-            for d in range(4):
-                def around(sp):
-                    x = state[b, d, sp, i, pl.ds(at + 8, RC)]
-                    low_x = state[b, d, sp, i - 1, pl.ds(at + 8, RC)]
-                    s = state[b, d, sp, i + 1, pl.ds(at + 8, RC)]
-                    s = s + state[b, d, sp, i, pl.ds(at + 7, RC)]
-                    s = s + state[b, d, sp, i, pl.ds(at + 9, RC)]
-                    s = s + jnp.where(first_lane, 0.0, pltpu.roll(x, 1, 1))
-                    s = s + jnp.where(last_lane, 0.0, pltpu.roll(x, 127, 1))
-                    return x, low_x, s
-
-                p, p_low, p_sum = around(0)
-                q, q_low, q_sum = around(1)
-                src = vfine[d, k, rows] * g + p * rb + q * ra
-                state[1 - b, d, 0, i, pl.ds(at + 8, RC)] = (
-                    0.27 * p + 0.08 * p_sum + 0.33 * p_low - src
-                )
-                state[1 - b, d, 1, i, pl.ds(at + 8, RC)] = (
-                    0.34 * q + 0.06 * q_sum + 0.31 * q_low + src
-                )
+    def rows_of(b, i, k, at):
+        rows = pl.ds(at, RC)
+        ra = coef[0, i, rows]
+        rb = coef[1, i, rows]
+        g = coef[2, i, rows]
+        for d in range(4):
+            def around(sp):
+                x = state[b, d, sp, i, pl.ds(at + 8, RC)]
+                low_x = state[b, d, sp, i - 1, pl.ds(at + 8, RC)]
+                s = state[b, d, sp, i + 1, pl.ds(at + 8, RC)]
+                s = s + state[b, d, sp, i, pl.ds(at + 7, RC)]
+                s = s + state[b, d, sp, i, pl.ds(at + 9, RC)]
+                s = s + jnp.where(first_lane, 0.0, pltpu.roll(x, 1, 1))
+                s = s + jnp.where(last_lane, 0.0, pltpu.roll(x, 127, 1))
+                return x, low_x, s
+
+            p, p_low, p_sum = around(0)
+            q, q_low, q_sum = around(1)
+            src = vfine[d, k, rows] * g + p * rb + q * ra
+            state[1 - b, d, 0, i, pl.ds(at + 8, RC)] = (
+                0.27 * p + 0.08 * p_sum + 0.33 * p_low - src
+            )
+            state[1 - b, d, 1, i, pl.ds(at + 8, RC)] = (
+                0.34 * q + 0.06 * q_sum + 0.31 * q_low + src
+            )
+
+    def planes(b, start, stop):
+        @pl.loop(start, stop)
+        def _(i):
+            k = (i + 1) // 2
+
+            @pl.loop(0, ROWS // (RC * PARTS))
+            def _(n):
+                for h in range(PARTS):
+                    rows_of(b, i, k, pl.multiple_of(n * (RC * PARTS) + h * RC, 8))
 
     def update(u):
-        @pl.loop(jnp.maximum(u - 1, low), jnp.minimum(15 - u, high))
-        def _(i):
-            plane(u % 2, i)
+        planes(u % 2, jnp.maximum(u - 1, low), jnp.minimum(15 - u, high))
 
     update(2)
+    args_b = (1, cand1, ring1, own1, ext1, z1_r, f1_s, f1_r)
+    sent_b = ring_step(*args_b, ORDER[:2])
     update(3)
-
-    sent_b = ring_step(1, cand1, ring1, own1, ext1, z1_r, f1_s, f1_r)
+    sent_b += ring_step(*args_b, ORDER[2:])
     part = pl.ds(2 - 2 * zl, 2)
     x1 = remote(ext1.at[0, :, part], ext1.at[1, :, part], x1_s, x1_r, xt)
     x1.start()
@@ -352,28 +384,27 @@
         )
         return here, there
 
-    srow = iota((64, 256), 0)
-    scol = iota((64, 256), 1) >> 2
-
     @pl.loop(0, 4)
     def _(i):
-        plane(0, 5 + i)
+        planes(0, 5 + i, 6 + i)
         here, there = out_copies(i)
         here.start()
         there.start()
-
-    smat = jnp.where(scol == 4 * (srow & 15) + (srow >> 4), 1.0 / 32.0, 0.0).astype(F32)
 
     @pl.loop(0, 8)
     def _(n):
         cp = n // 4
         d = n % 4
-        q = state[1, d, 1, 5 + 2 * cp, held] + state[1, d, 1, 6 + 2 * cp, held]
-        m = jnp.dot(smat, q, precision=HI, preferred_element_type=F32)
+        q = (state[1, d, 1, 5 + 2 * cp, held] + state[1, d, 1, 6 + 2 * cp, held]) * (1.0 / 32.0)
+        m = jnp.zeros((64, 128), F32)
+        for part in thirds(q):
+            m = m + jnp.dot(smat[...], part, preferred_element_type=F32)
         acc = jnp.zeros((16, 128), F32)
-        for jj in range(4):
-            t = jnp.where(k_out == 32 * jj + (k_in >> 2), 1.0, 0.0).astype(F32)
-            acc = acc + jnp.dot(m[16 * jj : 16 * jj + 16], t, precision=HI, preferred_element_type=F32)
+        for part in thirds(m):
+            for jj in range(4):
+                acc = acc + jnp.dot(
+                    part[16 * jj : 16 * jj + 16], tmat[jj], preferred_element_type=F32
+                )
         for g in range(4):
             means[d // 2, (d % 2) * 8 + cp * 4 + g] = acc[4 * g : 4 * g + 4]
 
@@ -468,8 +499,11 @@
         vmem((32, 4, 2, 2, 128), F32),
         vmem((32, 4, 2, 2, 128), F32),
         vmem((4, 8, 32, 128), F32),
-        vmem((128, 128), F32),
-        vmem((ROWS, 128), F32),
+        vmem((3, 128, 128), BF16),
+        vmem((ROWS, 128), BF16),
+        vmem((128, 512), BF16),
+        vmem((4, 128, 128), BF16),
+        vmem((64, 256), BF16),
         pltpu.SMEM((32,), jnp.int32),
         vmem((2, 16, 4, 128), F32),
         vmem((32, 4, 128), F32),

time: 168 us -> 126 us (0.75)
  Pallas kernels: 162 us -> 120 us
    pallas_call x1, Pallas kernels: 162 us -> 120 us  [local(): pl.pallas_call(sweep, out_shape=(jax.ShapeDtypeStruct((2, 2, 4, 512, 128)...]
where the time goes in v2:
time: 126 us
  Pallas kernels  120 us (95%)
  local copies, waits for them, and re-layouts  5.27 us (4%)
    pallas_call x1, Pallas kernels, local(): pl.pallas_call(sweep, out_shape=(jax.ShapeDtypeStruct((2, 2, 4, 512, 128)...  120 us
    unnamed x4, local copies, waits for them, and re-layouts  5.27 us

profile of v2, /device:TPU:0, one launch (start us, length us, event | category | flops | bytes accessed | tf_op | source)
XLA Modules:
  0.0 125.5 jit_solution(17949353476735208204)
XLA Ops:
  0.6 119.6 %sweep.1 = (f32[2,2,4,512,128]{4,3,2,1,0:T(8,128)}, f32[2,2,2,4,4,128]{5,4,3,2,1,0:T(4,128)}) custom-call(s32[4]{0:T(128)} %owner.1, s32[32]{0:T(128)} %block.1, f32[1,2,4,512,128]{4,3,2,1,0:T(8,128)} %store.1, f32[4,512,128]{2,1,0:T(8,128)} %rate.1, f32[2,32,2,128]{3,2,1,0:T(2,128)} %bitcast.2), custom_call_target="tpu_custom_call" | custom-call | tf_op jit(solution)/shard_map/sweep/pallas_call | solution.py:518
  120.2 0.0 copy-start
  120.3 4.6 %copy.10 = f32[2,2,4,512,128]{4,3,2,1,0:T(8,128)} copy(f32[2,2,4,512,128]{4,3,2,1,0:T(8,128)} %get-tuple-element.10) | data formatting | bytes 8388608
  124.9 0.0 copy-done
  124.9 0.6 copy.11
Async XLA Ops:
  120.2 4.6 %copy-start = (f32[2,2,2,4,4,128]{5,4,3,2,1,0:T(4,128)S(1)}, f32[2,2,2,4,4,128]{5,4,3,2,1,0:T(4,128)}, u32[]{:S(2)}) copy-start(f32[2,2,2,4,4,128]{5,4,3,2,1,0:T(4,128)} %get-tuple-element.5) | copy-start | bytes 196612
